TPU v7x, 256 devices: a whole 4x4x8 slice. The times are simulated.
256 devices in a mesh: rows: 64 (over x_lo, y, z), cols: 4 (over x_hi, core).
Axes of the slice: x: 4 (x_hi: 2, x_lo: 2; x = x_hi * 2 + x_lo), y: 4, z: 8, core: 2. Of those that a mesh axis runs over, the one named last changes fastest.
Arguments:
- l_blocks: bfloat16 [2048, 64, 1920], P(('rows', 'cols')), may hold values from -0.25 to 0.25
- s_blocks: bfloat16 [2048, 64, 1280], P('rows', None, 'cols'), may hold values from -6 to 6
- l_index: int32 [2048, 30], P(('rows', 'cols')), may hold values from 0 to 2047, as said below
- s_cols: int32 [2048, 20], replicated, may hold values from 0 to 2047, as said below
- c_index: int32 [2048, 24], P(('rows', 'cols')), may hold values from 0 to 2047, as said below
Outputs:
- product: bfloat16 [2048, 64, 1536], P(('rows', 'cols'))
Inputs may be any that keep to these rules, and one draw needn't show every extreme that they name: `l_index`: the 30 entries of block-row i are distinct and lie in the window of 31 block-rows starting at max(0, min(i - 15, 2017)). `s_cols`: the entries of one block-row are distinct; those in slots p * 5 to (p + 1) * 5 - 1 are congruent to p modulo 20 // 5 and lie within 7 such columns around the block-row. `c_index`: the entries of one block-row are distinct; those in slots p * 6 to (p + 1) * 6 - 1 are congruent to p modulo 24 // 6 and lie within 16 such columns around the block-row.
All inputs are finite; a program needn't handle non-finite values.
Results may differ from a plain program's by a relative error of at most 0.001.
Values may be sent and summed in bfloat16 or wider, within the bound.
No kernel may reach another device: no remote copies, remote signals or barrier semaphores. Data moves between devices by JAX's collectives and lax.ppermute only.
A program may use at most 192 MiB of HBM per device.

v0:
```python
import math
import jax
import jax.numpy as jnp
from jax import lax
from jax.sharding import PartitionSpec as P

HL = 15


def padded(block, sides, width):
    for axis, dim in sides:
        count = lax.axis_size(axis)
        forward = [(i, i + 1) for i in range(count - 1)]
        backward = [(target, source) for source, target in forward]
        low = lax.ppermute(
            lax.slice_in_dim(block, block.shape[dim] - width, None, axis=dim), axis, forward
        )
        high = lax.ppermute(lax.slice_in_dim(block, 0, width, axis=dim), axis, backward)
        block = jnp.concatenate([low, block, high], axis=dim)
    return block


def row_products(l_rows, l_ids, want_index, s_near, slot_cols, first):
    total = l_rows.shape[0]
    width = l_rows.shape[1]
    slot_total = s_near.shape[2] // width
    kept = want_index.shape[1]
    s_four = s_near.reshape(s_near.shape[0], width, slot_total, width)
    s_four = jnp.concatenate(
        [s_four, jnp.zeros((s_four.shape[0], width, 1, width), s_four.dtype)], axis=2
    )
    per_turn = math.gcd(total, max(1, 96 // kept))

    def single(left_row, left_ids, want_cols):
        slot_ids = jnp.take(slot_cols, left_ids, axis=0)
        match = slot_ids[:, None, :] == want_cols[None, :, None]
        slot_pick = jnp.sum(
            jnp.where(match, lax.iota(jnp.int32, slot_total)[None, None, :], 0),
            axis=2,
            dtype=jnp.int32,
        )
        found = jnp.any(match, axis=2)
        slot_pick = jnp.where(found, slot_pick, slot_total)
        local_ids = left_ids - first
        picked = s_four[local_ids[:, None], :, slot_pick, :]
        left_three = left_row.reshape(width, left_ids.shape[0], width)
        summed = jnp.einsum("akb,kmbc->amc", left_three, picked, preferred_element_type=jnp.float32)
        return summed.reshape(width, kept * width).astype(jnp.bfloat16)

    def one_group(group):
        return jax.vmap(single)(group[0], group[1], group[2])

    shaped = tuple(
        (
            a.reshape((total // per_turn, per_turn) + a.shape[1:])
            for a in (l_rows, l_ids, want_index)
        )
    )
    result = lax.map(one_group, shaped)
    return result.reshape((total,) + result.shape[2:])


def shards(l_blocks, s_blocks, l_index, s_cols, c_index):
    row_here = lax.axis_index("rows")
    group_size = s_blocks.shape[0]
    group_first = row_here * group_size
    whole = lax.all_gather(s_blocks, "cols", axis=2, tiled=True)
    nearby = padded(whole, (("rows", 0),), HL)
    return row_products(l_blocks, l_index, c_index, nearby, s_cols, group_first - HL)


def solution(mesh):
    return jax.shard_map(
        shards,
        mesh=mesh,
        in_specs=(
            P(("rows", "cols"), None, None),
            P("rows", None, "cols"),
            P(("rows", "cols"), None),
            P(),
            P(("rows", "cols"), None),
        ),
        out_specs=P(("rows", "cols"), None, None),
        check_vma=False,
    )
```

profile of v0, /device:TPU:2, one launch (start us, length us, event | category | flops | bytes accessed | tf_op | source)
XLA Modules:
  0.0 386.1 jit_solution(16272070342322603991)
XLA Ops:
  6.5 0.0 all-gather.2.cloned.1.call-start
  6.5 5.9 %copy.44 = bf16[32,64,320]{1,0,2:T(8,128)(2,1)} copy(bf16[32,64,320]{2,1,0:T(8,128)(2,1)} %param.8) | data formatting | bytes 2621440 | tf_op args[1]
  12.4 0.0 all-gather.2.cloned.1.call-update
  12.5 79.0 %all-gather.2.cloned.1.call-done = bf16[32,64,1280]{1,0,2:T(8,128)(2,1)} async-done(((bf16[32,64,320]{1,0,2:T(8,128)(2,1)}), bf16[32,64,1280]{1,0,2:T(8,128)(2,1)}) %all-gather.2.cloned.1.call-update) | async-done | bytes 5242896 | tf_op jit(solution)/shard_map/all_gather | solution.py:67
  91.4 9.8 %fusion.13 = (bf16[15,64,1280]{1,0,2:T(8,128)(2,1)}, bf16[15,64,1280]{1,0,2:T(8,128)(2,1)}) fusion(bf16[32,64,1280]{1,0,2:T(8,128)(2,1)} %all-gather.2.cloned.1.call-done), kind=kLoop, calls=%fused_computation.26 | loop fusion | bytes 9830400 | tf_op jit(solution)/shard_map/slice | solution.py:16
  101.2 7.1 %copy.45 = bf16[15,64,1280]{2,1,0:T(8,128)(2,1)} copy(bf16[15,64,1280]{1,0,2:T(8,128)(2,1)} %get-tuple-element.104) | data formatting | bytes 4915200 | tf_op jit(solution)/shard_map/slice | solution.py:16
  108.3 3.5 collective-permute-start
  111.8 0.0 copy-start.1
  111.8 7.1 %copy.46 = bf16[15,64,1280]{2,1,0:T(8,128)(2,1)} copy(bf16[15,64,1280]{1,0,2:T(8,128)(2,1)} %get-tuple-element.105) | data formatting | bytes 4915200 | tf_op jit(solution)/shard_map/slice | solution.py:18
  118.9 6.9 %collective-permute-start.1 = (bf16[15,64,1280]{2,1,0:T(8,128)(2,1)}, bf16[15,64,1280]{2,1,0:T(8,128)(2,1)}, u32[]{:S(2)}, u32[]{:S(2)}) collective-permute-start(bf16[15,64,1280]{2,1,0:T(8,128)(2,1)} %copy.46), channel_id=1, source_target_pairs={{4,0},{8,4},{12,8},{16,12},{20,16},{24,20},{28,24},{32,28},{36,32}... | collective-permute-start | bytes 7372808 | tf_op jit(solution)/shard_map/ppermute | solution.py:18
  125.9 0.0 copy-done.1
  125.9 1.4 copy.48
  127.2 12.7 %copy.47 = bf16[32,64,1280]{2,1,0:T(8,128)(2,1)} copy(bf16[32,64,1280]{1,0,2:T(8,128)(2,1)} %all-gather.2.cloned.1.call-done) | data formatting | bytes 10485760 | tf_op jit(solution)/shard_map/all_gather | solution.py:67
  139.9 30.7 %collective-permute-done = bf16[15,64,1280]{2,1,0:T(8,128)(2,1)S(1)} collective-permute-done((bf16[15,64,1280]{2,1,0:T(8,128)(2,1)}, bf16[15,64,1280]{2,1,0:T(8,128)(2,1)S(1)}, u32[]{:S(2)}, u32[]{:S(2)}) %collective-permute-start) | collective-permute-done | bytes 2457632 | tf_op jit(solution)/shard_map/ppermute | solution.py:15
  170.6 8.4 %collective-permute-done.1 = bf16[15,64,1280]{2,1,0:T(8,128)(2,1)} collective-permute-done((bf16[15,64,1280]{2,1,0:T(8,128)(2,1)}, bf16[15,64,1280]{2,1,0:T(8,128)(2,1)}, u32[]{:S(2)}, u32[]{:S(2)}) %collective-permute-start.1) | collective-permute-done | bytes 2457632 | tf_op jit(solution)/shard_map/ppermute | solution.py:18
  179.0 8.8 %pad_maximum_fusion = bf16[62,64,1280]{2,1,0:T(8,128)(2,1)} fusion(bf16[15,64,1280]{2,1,0:T(8,128)(2,1)} %collective-permute-done.1, bf16[32,64,1280]{2,1,0:T(8,128)(2,1)} %copy.47, bf16[15,64,1280]{2,1,0:T(8,128)(2,1)S(1)} %collective-permute-done), kind=kLoop, calls=%fused_computation.25 | loop fusion | flops 10158080 | bytes 20316160 | tf_op jit(solution)/shard_map/concatenate | solution.py:19
  187.9 29.2 %reshape.109 = bf16[62,64,20,64]{3,2,1,0:T(8,128)(2,1)} reshape(bf16[62,64,1280]{2,1,0:T(8,128)(2,1)} %pad_maximum_fusion) | data formatting | bytes 20316160 | tf_op jit(solution)/shard_map/reshape | solution.py:28
  217.0 12.8 %copy.54 = bf16[62,64,20,64]{3,1,2,0:T(8,128)(2,1)S(1)} copy(bf16[62,64,20,64]{3,2,1,0:T(8,128)(2,1)} %reshape.109) | data formatting | bytes 20316160
  229.8 0.0 copy-start
  229.8 0.0 copy-start.2
  229.8 11.0 %concatenate.10.clone = bf16[62,64,21,64]{3,1,2,0:T(8,128)(2,1)} pad(bf16[62,64,20,64]{3,1,2,0:T(8,128)(2,1)S(1)} %copy.54, bf16[]{:T(256)} %constant.33.clone.1), padding=0_0x0_0x0_1x0_0 | pad | bytes 20824066 | tf_op jit(solution)/shard_map/concatenate | solution.py:29
  240.8 0.0 copy-done
  240.8 0.0 copy-done.2
  240.8 138.4 %while.10 = (s32[]{:T(128)}, bf16[2,4,64,1536]{3,2,1,0:T(8,128)(2,1)}, bf16[2,4,64,1920]{3,2,1,0:T(8,128)(2,1)}, s32[2,4,30]{2,1,0:T(4,128)S(1)}, s32[]{:T(128)}...) while((s32[]{:T(128)}, ...), condition=%wide.region_3.4_spmd, body=%wide.region_0.3_spmd.sunk | while | flops 1510650240 | bytes 81435040 | solution.py:59
  240.8 0.1 reshape.140
  240.9 1.9 gather_fusion
  242.8 0.1 copy.71
  242.9 0.1 reshape.141
  243.1 0.2 fusion.21
  243.2 0.2 compare_reduce_fusion.2
  243.5 0.1 copy.73
  243.6 0.1 reshape.142
  243.7 39.2 %gather_fusion.1 = bf16[2880,64,64]{2,1,0:T(8,128)(2,1)} fusion(bf16[62,64,21,64]{3,1,2,0:T(8,128)(2,1)} %get-tuple-element.180, s32[2880]{0:T(1024)S(1)} %reshape.142), kind=kCustom, calls=%fused_computation.1.clone.1 | custom fusion | bytes 47208960 | tf_op jit(solution)/shard_map/while/body/eval_jaxpr/vmap()/gather | solution.py:45
  282.9 1.3 constant_dynamic-slice_fusion.2
  284.2 2.1 reshape.143
  286.3 19.4 %bitcast_convert_fusion.2 = bf16[4,64,24,64]{3,1,2,0:T(8,128)(2,1)} fusion(bf16[4,30,24,64,64]{4,3,2,1,0:T(8,128)(2,1)} %bitcast.48, bf16[4,64,30,64,1]{3,2,1,0,4:T(8,128)(2,1)S(1)} %bitcast.49), kind=kOutput, calls=%fused_computation.4.clone.1 | convolution fusion | flops 1510342656 | bytes 25362432 | tf_op jit(solution)/shard_map/while/body/eval_jaxpr/vmap(akb,kmbc->amc)/dot_general | solution.py:47
  305.7 2.4 copy.74
  308.1 1.0 convert_element_type.17
  309.1 0.9 constant_dynamic-update-slice_fusion.2
  310.0 0.1 reshape.140
  310.1 1.9 gather_fusion
  312.0 0.1 copy.71
  312.1 0.1 reshape.141
  312.3 0.2 fusion.21
  312.4 0.2 compare_reduce_fusion.2
  312.7 0.1 copy.73
  312.8 0.1 reshape.142
  312.9 39.2 %gather_fusion.1 = bf16[2880,64,64]{2,1,0:T(8,128)(2,1)} fusion(bf16[62,64,21,64]{3,1,2,0:T(8,128)(2,1)} %get-tuple-element.180, s32[2880]{0:T(1024)S(1)} %reshape.142), kind=kCustom, calls=%fused_computation.1.clone.1 | custom fusion | bytes 47208960 | tf_op jit(solution)/shard_map/while/body/eval_jaxpr/vmap()/gather | solution.py:45
  352.1 1.3 constant_dynamic-slice_fusion.2
  353.4 2.1 reshape.143
  355.5 19.4 %bitcast_convert_fusion.2 = bf16[4,64,24,64]{3,1,2,0:T(8,128)(2,1)} fusion(bf16[4,30,24,64,64]{4,3,2,1,0:T(8,128)(2,1)} %bitcast.48, bf16[4,64,30,64,1]{3,2,1,0,4:T(8,128)(2,1)S(1)} %bitcast.49), kind=kOutput, calls=%fused_computation.4.clone.1 | convolution fusion | flops 1510342656 | bytes 25362432 | tf_op jit(solution)/shard_map/while/body/eval_jaxpr/vmap(akb,kmbc->amc)/dot_general | solution.py:47
  374.9 2.4 copy.74
  377.3 1.0 convert_element_type.17
  378.3 0.9 constant_dynamic-update-slice_fusion.2
  (17 shorter events, 0.2 us)
Async XLA Ops:
  6.5 84.9 %all-gather.2.cloned.1.call-start = ((), (), s32[]{:S(2)}) async-start(), calls=%async_computation | async-start | bytes 13107200 | tf_op jit(solution)/shard_map/all_gather | solution.py:67
  108.3 62.3 %collective-permute-start = (bf16[15,64,1280]{2,1,0:T(8,128)(2,1)}, bf16[15,64,1280]{2,1,0:T(8,128)(2,1)S(1)}, u32[]{:S(2)}, u32[]{:S(2)}) collective-permute-start(bf16[15,64,1280]{2,1,0:T(8,128)(2,1)} %copy.45), channel_id=1, source_target_pairs={{0,4},{4,8},{8,12},{12,16},{16,20},{20,24},{24,28},{28,32},{32,36}... | collective-permute-start | bytes 7372808 | tf_op jit(solution)/shard_map/ppermute | solution.py:15
  111.8 14.1 %copy-start.1 = (s32[2048,20]{0,1:T(8,128)S(1)}, s32[2048,20]{0,1:T(8,128)}, u32[]{:S(2)}) copy-start(s32[2048,20]{0,1:T(8,128)} %param.10) | copy-start | bytes 491524
  118.9 60.1 %collective-permute-start.1 = (bf16[15,64,1280]{2,1,0:T(8,128)(2,1)}, bf16[15,64,1280]{2,1,0:T(8,128)(2,1)}, u32[]{:S(2)}, u32[]{:S(2)}) collective-permute-start(bf16[15,64,1280]{2,1,0:T(8,128)(2,1)} %copy.46), channel_id=1, source_target_pairs={{4,0},{8,4},{12,8},{16,12},{20,16},{24,20},{28,24},{32,28},{36,32}... | collective-permute-start | bytes 7372808 | tf_op jit(solution)/shard_map/ppermute | solution.py:18
  229.8 11.0 %copy-start = (s32[8,30]{1,0:T(8,128)S(1)}, s32[8,30]{1,0:T(8,128)}, u32[]{:S(2)}) copy-start(s32[8,30]{1,0:T(8,128)} %param.9) | copy-start | bytes 2884
  229.8 11.0 %copy-start.2 = (s32[8,24]{1,0:T(8,128)S(1)}, s32[8,24]{1,0:T(8,128)}, u32[]{:S(2)}) copy-start(s32[8,24]{1,0:T(8,128)} %param.11) | copy-start | bytes 2308
Sparse Core Ops, SparseCore 0:
  12.6 78.8 all-gather.1
where the time goes:
time: 388 us; the launch traced here: 386 us
  local copies, waits for them, and re-layouts  195 us (50%)
  waiting for transfers between devices  118 us (30%)
  matrix products  38.7 us (10%)
  between operations  13.5 us (3%)
  starting transfers between devices  10.4 us (3%)
  other arithmetic  9.79 us (3%)
    all_gather x1, waiting for transfers between devices, shards(): whole = lax.all_gather(s_blocks, 'cols', axis=2, tiled=True)  79 us
    gather x2, local copies, waits for them, and re-layouts, single(): picked = s_four[local_ids[:, None], :, slot_pick, :]  78.4 us
    dot_general x2, matrix products, single(): jnp.einsum('akb,kmbc->amc', left_three, picked, preferred_element_type=jn...  38.7 us
    ppermute x1, waiting for transfers between devices, padded(): lax.ppermute(lax.slice_in_dim(block, block.shape[dim] - width, None, axis...  30.7 us
    reshape x1, local copies, waits for them, and re-layouts, row_products(): s_four = s_near.reshape(s_near.shape[0], width, slot_total, width)  29.2 us
    unnamed x8, local copies, waits for them, and re-layouts  18.7 us
    slice x2, local copies, waits for them, and re-layouts, padded(): lax.slice_in_dim(block, block.shape[dim] - width, None, axis=dim)  16.9 us
    all_gather x1, local copies, waits for them, and re-layouts, shards(): whole = lax.all_gather(s_blocks, 'cols', axis=2, tiled=True)  12.7 us
  transfers between devices with their start and end apart: 3, of which 3 were waited for; matrix products, arithmetic and copies ran while one was open for 5% of the time, Pallas kernels for 0%

commit v1 on v0

--- a/solution.py
+++ b/solution.py
@@ -64,7 +64,9 @@
     row_here = lax.axis_index("rows")
     group_size = s_blocks.shape[0]
     group_first = row_here * group_size
-    whole = lax.all_gather(s_blocks, "cols", axis=2, tiled=True)
+    whole = jnp.concatenate(
+        lax.all_to_all(jnp.stack([s_blocks] * lax.axis_size("cols")), "cols", 0, 0), axis=2
+    )
     nearby = padded(whole, (("rows", 0),), HL)
     return row_products(l_blocks, l_index, c_index, nearby, s_cols, group_first - HL)
 

time: 388 us -> 358 us (0.923)
  waiting for transfers between devices: 118 us -> 13.7 us
  blocking collectives: 0 us -> 75.3 us
  between operations: 13.5 us -> 0.09 us
  other arithmetic: 9.79 us -> 22.8 us
    all_gather x1 -> x0, waiting for transfers between devices: 79 us -> none  [shards(): whole = lax.all_gather(s_blocks, 'cols', axis=2, tiled=True)]
    all_to_all x0 -> x1, blocking collectives: none -> 75.3 us  [shards(): lax.all_to_all(jnp.stack([s_blocks] * lax.axis_size('cols')), 'cols', 0, 0)]
    concatenate x0 -> x3, local copies, waits for them, and re-layouts: none -> 33.8 us  [padded(): block = jnp.concatenate([low, block, high], axis=dim)]
    ppermute x1, waiting for transfers between devices: 30.7 us -> 12.2 us  [padded(): lax.ppermute(lax.slice_in_dim(block, block.shape[dim] - width, None, axis...]
    reshape x1, local copies, waits for them, and re-layouts: 29.2 us -> 11.3 us  [shards(): jnp.concatenate(lax.all_to_all(jnp.stack([s_blocks] * lax.axis_size('cols...]
    concatenate x1, other arithmetic: 8.84 us -> 21.9 us  [padded(): block = jnp.concatenate([low, block, high], axis=dim)]
    all_gather x1 -> x0, local copies, waits for them, and re-layouts: 12.7 us -> none  [shards(): whole = lax.all_gather(s_blocks, 'cols', axis=2, tiled=True)]
    ppermute x1, waiting for transfers between devices: 8.41 us -> 1.52 us  [padded(): lax.ppermute(lax.slice_in_dim(block, 0, width, axis=dim), axis, backward)]
  transfers between devices with their start and end apart: 3 -> 2, of which waited for: 3 -> 2; matrix products, arithmetic and copies ran while one was open for 5% -> 13% of each run, Pallas kernels for 0% -> 0%
where the time goes in v1:
time: 358 us; the launch traced here: 356 us
  local copies, waits for them, and re-layouts  192 us (54%)
  blocking collectives  75.3 us (21%)
  matrix products  38.7 us (11%)
  other arithmetic  22.8 us (6%)
  waiting for transfers between devices  13.7 us (4%)
  starting transfers between devices  13.2 us (4%)
    gather x2, local copies, waits for them, and re-layouts, single(): picked = s_four[local_ids[:, None], :, slot_pick, :]  78.4 us
    all_to_all x1, blocking collectives, shards(): lax.all_to_all(jnp.stack([s_blocks] * lax.axis_size('cols')), 'cols', 0, 0)  75.3 us
    dot_general x2, matrix products, single(): jnp.einsum('akb,kmbc->amc', left_three, picked, preferred_element_type=jn...  38.7 us
    concatenate x3, local copies, waits for them, and re-layouts, padded(): block = jnp.concatenate([low, block, high], axis=dim)  33.8 us
    concatenate x1, other arithmetic, padded(): block = jnp.concatenate([low, block, high], axis=dim)  21.9 us
    unnamed x9, local copies, waits for them, and re-layouts  14.6 us
    ppermute x1, waiting for transfers between devices, padded(): lax.ppermute(lax.slice_in_dim(block, block.shape[dim] - width, None, axis...  12.2 us
    reshape x1, local copies, waits for them, and re-layouts, shards(): jnp.concatenate(lax.all_to_all(jnp.stack([s_blocks] * lax.axis_size('cols...  11.3 us
  transfers between devices with their start and end apart: 2, of which 2 were waited for; matrix products, arithmetic and copies ran while one was open for 13% of the time, Pallas kernels for 0%

profile of v1, /device:TPU:2, one launch (start us, length us, event | category | flops | bytes accessed | tf_op | source)
XLA Modules:
  0.0 356.5 jit_solution(5977913841004731016)
XLA Ops:
  0.0 2.5 stack.2
  2.5 75.3 %all_to_all.5 = bf16[4,32,64,320]{3,2,1,0:T(8,128)(2,1)S(1)} all-to-all(bf16[4,32,64,320]{3,2,1,0:T(8,128)(2,1)S(1)} %stack.2), channel_id=1, replica_groups=mesh['rows'=64,'cols'=4] {'cols'}, dimensions={0} | all-to-all | bytes 10485760 | tf_op jit(solution)/shard_map/all_to_all | solution.py:68
  77.8 0.0 copy-start
  77.8 0.8 fusion.13
  78.6 1.8 copy-done
  80.5 4.0 %copy.42 = bf16[15,64,4,320]{3,2,1,0:T(4,128)(2,1)} copy(bf16[15,64,4,320]{3,1,0,2:T(8,128)(2,1)S(1)} %get-tuple-element.104) | data formatting | bytes 4915200 | tf_op jit(solution)/shard_map/slice | solution.py:16
  84.5 5.9 %slice.13 = bf16[15,64,1280]{2,1,0:T(8,128)(2,1)} reshape(bf16[15,64,4,320]{3,2,1,0:T(4,128)(2,1)} %copy.42) | data formatting | bytes 4915200 | tf_op jit(solution)/shard_map/slice | solution.py:16
  90.4 3.8 %collective-permute-start = (bf16[15,64,1280]{2,1,0:T(8,128)(2,1)}, bf16[15,64,1280]{2,1,0:T(8,128)(2,1)}, u32[]{:S(2)}, u32[]{:S(2)}) collective-permute-start(bf16[15,64,1280]{2,1,0:T(8,128)(2,1)} %slice.13), channel_id=1, source_target_pairs={{0,4},{4,8},{8,12},{12,16},{16,20},{20,24},{24,28},{28,32},{32,36}... | collective-permute-start | bytes 7372808 | tf_op jit(solution)/shard_map/ppermute | solution.py:15
  94.2 4.0 %copy.44 = bf16[15,64,4,320]{3,2,1,0:T(4,128)(2,1)} copy(bf16[15,64,4,320]{3,1,0,2:T(8,128)(2,1)S(1)} %get-tuple-element.105) | data formatting | bytes 4915200 | tf_op jit(solution)/shard_map/slice | solution.py:18
  98.2 0.0 copy-start.2
  98.2 4.7 %slice.15 = bf16[15,64,1280]{2,1,0:T(8,128)(2,1)S(1)} reshape(bf16[15,64,4,320]{3,2,1,0:T(4,128)(2,1)} %copy.44) | data formatting | bytes 4915200 | tf_op jit(solution)/shard_map/slice | solution.py:18
  103.0 9.4 %collective-permute-start.1 = (bf16[15,64,1280]{2,1,0:T(8,128)(2,1)S(1)}, bf16[15,64,1280]{2,1,0:T(8,128)(2,1)}, u32[]{:S(2)}, u32[]{:S(2)}) collective-permute-start(bf16[15,64,1280]{2,1,0:T(8,128)(2,1)S(1)} %slice.15), channel_id=1, source_target_pairs={{4,0},{8,4},{12,8},{16,12},{20,16},{24,20},{28,24},{32,28},{36,32}... | collective-permute-start | bytes 7372808 | tf_op jit(solution)/shard_map/ppermute | solution.py:18
  112.4 0.0 copy-done.2
  112.4 1.3 copy.45
  113.7 11.3 %copy.43 = bf16[32,64,4,320]{3,2,1,0:T(4,128)(2,1)} copy(bf16[32,64,4,320]{3,1,0,2:T(8,128)(2,1)} %bitcast.51) | data formatting | bytes 10485760 | tf_op jit(solution)/shard_map/reshape | solution.py:67
  125.0 17.6 %concatenate.17 = bf16[32,64,20,64]{3,2,1,0:T(8,128)(2,1)} reshape(bf16[32,64,4,320]{3,2,1,0:T(4,128)(2,1)} %copy.43) | data formatting | bytes 10485760 | tf_op jit(solution)/shard_map/concatenate | solution.py:19
  142.6 12.2 %collective-permute-done = bf16[15,64,1280]{2,1,0:T(8,128)(2,1)} collective-permute-done((bf16[15,64,1280]{2,1,0:T(8,128)(2,1)}, bf16[15,64,1280]{2,1,0:T(8,128)(2,1)}, u32[]{:S(2)}, u32[]{:S(2)}) %collective-permute-start) | collective-permute-done | bytes 2457632 | tf_op jit(solution)/shard_map/ppermute | solution.py:15
  154.8 8.1 %concatenate.16 = bf16[15,64,20,64]{3,2,1,0:T(8,128)(2,1)} reshape(bf16[15,64,1280]{2,1,0:T(8,128)(2,1)} %collective-permute-done) | data formatting | bytes 4915200 | tf_op jit(solution)/shard_map/concatenate | solution.py:19
  162.9 1.5 collective-permute-done.1
  164.4 8.1 %concatenate.18 = bf16[15,64,20,64]{3,2,1,0:T(8,128)(2,1)} reshape(bf16[15,64,1280]{2,1,0:T(8,128)(2,1)} %collective-permute-done.1) | data formatting | bytes 4915200 | tf_op jit(solution)/shard_map/concatenate | solution.py:19
  172.5 21.9 %pad_maximum_fusion = bf16[62,64,20,64]{3,2,1,0:T(8,128)(2,1)} fusion(bf16[15,64,20,64]{3,2,1,0:T(8,128)(2,1)} %concatenate.18, bf16[32,64,20,64]{3,2,1,0:T(8,128)(2,1)} %concatenate.17, bf16[15,64,20,64]{3,2,1,0:T(8,128)(2,1)} %concatenate.16), kind=kLoop, calls=%fused_computation.25 | loop fusion | flops 10158080 | bytes 20316160 | tf_op jit(solution)/shard_map/concatenate | solution.py:19
  194.4 12.8 %copy.51 = bf16[62,64,20,64]{3,1,2,0:T(8,128)(2,1)S(1)} copy(bf16[62,64,20,64]{3,2,1,0:T(8,128)(2,1)} %pad_maximum_fusion) | data formatting | bytes 20316160
  207.1 0.0 copy-start.1
  207.2 0.0 copy-start.3
  207.2 10.9 %concatenate.20.clone = bf16[62,64,21,64]{3,1,2,0:T(8,128)(2,1)} pad(bf16[62,64,20,64]{3,1,2,0:T(8,128)(2,1)S(1)} %copy.51, bf16[]{:T(256)} %constant.33.clone.1), padding=0_0x0_0x0_1x0_0 | pad | bytes 20824066 | tf_op jit(solution)/shard_map/concatenate | solution.py:29
  218.1 0.0 copy-done.1
  218.1 0.0 copy-done.3
  218.1 138.4 %while.10 = (s32[]{:T(128)}, bf16[2,4,64,1536]{3,2,1,0:T(8,128)(2,1)}, bf16[2,4,64,1920]{3,2,1,0:T(8,128)(2,1)}, s32[2,4,30]{2,1,0:T(4,128)S(1)}, s32[]{:T(128)}...) while((s32[]{:T(128)}, ...), condition=%wide.region_3.4_spmd, body=%wide.region_0.3_spmd.sunk | while | flops 1510650240 | bytes 81435040 | solution.py:59
  218.1 0.1 reshape.150
  218.2 1.9 gather_fusion
  220.1 0.1 copy.68
  220.1 0.1 reshape.151
  220.3 0.2 fusion.21
  220.5 0.2 compare_reduce_fusion.2
  220.8 0.1 copy.70
  220.9 0.1 reshape.152
  221.0 39.2 %gather_fusion.1 = bf16[2880,64,64]{2,1,0:T(8,128)(2,1)} fusion(bf16[62,64,21,64]{3,1,2,0:T(8,128)(2,1)} %get-tuple-element.180, s32[2880]{0:T(1024)S(1)} %reshape.152), kind=kCustom, calls=%fused_computation.1.clone.1 | custom fusion | bytes 47208960 | tf_op jit(solution)/shard_map/while/body/eval_jaxpr/vmap()/gather | solution.py:45
  260.2 1.3 constant_dynamic-slice_fusion.2
  261.4 2.1 reshape.153
  263.6 19.4 %bitcast_convert_fusion.2 = bf16[4,64,24,64]{3,1,2,0:T(8,128)(2,1)} fusion(bf16[4,30,24,64,64]{4,3,2,1,0:T(8,128)(2,1)} %bitcast.49, bf16[4,64,30,64,1]{3,2,1,0,4:T(8,128)(2,1)S(1)} %bitcast.52), kind=kOutput, calls=%fused_computation.4.clone.1 | convolution fusion | flops 1510342656 | bytes 25362432 | tf_op jit(solution)/shard_map/while/body/eval_jaxpr/vmap(akb,kmbc->amc)/dot_general | solution.py:47
  283.0 2.4 copy.71
  285.4 1.0 convert_element_type.17
  286.4 0.9 constant_dynamic-update-slice_fusion.2
  287.3 0.1 reshape.150
  287.4 1.9 gather_fusion
  289.3 0.1 copy.68
  289.3 0.1 reshape.151
  289.5 0.2 fusion.21
  289.7 0.2 compare_reduce_fusion.2
  290.0 0.1 copy.70
  290.1 0.1 reshape.152
  290.2 39.2 %gather_fusion.1 = bf16[2880,64,64]{2,1,0:T(8,128)(2,1)} fusion(bf16[62,64,21,64]{3,1,2,0:T(8,128)(2,1)} %get-tuple-element.180, s32[2880]{0:T(1024)S(1)} %reshape.152), kind=kCustom, calls=%fused_computation.1.clone.1 | custom fusion | bytes 47208960 | tf_op jit(solution)/shard_map/while/body/eval_jaxpr/vmap()/gather | solution.py:45
  329.4 1.3 constant_dynamic-slice_fusion.2
  330.6 2.1 reshape.153
  332.8 19.4 %bitcast_convert_fusion.2 = bf16[4,64,24,64]{3,1,2,0:T(8,128)(2,1)} fusion(bf16[4,30,24,64,64]{4,3,2,1,0:T(8,128)(2,1)} %bitcast.49, bf16[4,64,30,64,1]{3,2,1,0,4:T(8,128)(2,1)S(1)} %bitcast.52), kind=kOutput, calls=%fused_computation.4.clone.1 | convolution fusion | flops 1510342656 | bytes 25362432 | tf_op jit(solution)/shard_map/while/body/eval_jaxpr/vmap(akb,kmbc->amc)/dot_general | solution.py:47
  352.1 2.4 copy.71
  354.6 1.0 convert_element_type.17
  355.6 0.9 constant_dynamic-update-slice_fusion.2
  (17 shorter events, 0.2 us)
Async XLA Ops:
  77.8 2.6 copy-start
  90.4 64.4 %collective-permute-start = (bf16[15,64,1280]{2,1,0:T(8,128)(2,1)}, bf16[15,64,1280]{2,1,0:T(8,128)(2,1)}, u32[]{:S(2)}, u32[]{:S(2)}) collective-permute-start(bf16[15,64,1280]{2,1,0:T(8,128)(2,1)} %slice.13), channel_id=1, source_target_pairs={{0,4},{4,8},{8,12},{12,16},{16,20},{20,24},{24,28},{28,32},{32,36}... | collective-permute-start | bytes 7372808 | tf_op jit(solution)/shard_map/ppermute | solution.py:15
  98.2 14.1 %copy-start.2 = (s32[2048,20]{0,1:T(8,128)S(1)}, s32[2048,20]{0,1:T(8,128)}, u32[]{:S(2)}) copy-start(s32[2048,20]{0,1:T(8,128)} %param.10) | copy-start | bytes 491524
  103.0 61.4 %collective-permute-start.1 = (bf16[15,64,1280]{2,1,0:T(8,128)(2,1)S(1)}, bf16[15,64,1280]{2,1,0:T(8,128)(2,1)}, u32[]{:S(2)}, u32[]{:S(2)}) collective-permute-start(bf16[15,64,1280]{2,1,0:T(8,128)(2,1)S(1)} %slice.15), channel_id=1, source_target_pairs={{4,0},{8,4},{12,8},{16,12},{20,16},{24,20},{28,24},{32,28},{36,32}... | collective-permute-start | bytes 7372808 | tf_op jit(solution)/shard_map/ppermute | solution.py:18
  207.1 10.9 %copy-start.1 = (s32[8,30]{1,0:T(8,128)S(1)}, s32[8,30]{1,0:T(8,128)}, u32[]{:S(2)}) copy-start(s32[8,30]{1,0:T(8,128)} %param.9) | copy-start | bytes 2884
  207.2 10.9 %copy-start.3 = (s32[8,24]{1,0:T(8,128)S(1)}, s32[8,24]{1,0:T(8,128)}, u32[]{:S(2)}) copy-start(s32[8,24]{1,0:T(8,128)} %param.11) | copy-start | bytes 2308
